TPU v7x, 32 devices: a whole 2x2x4 slice. The times are simulated.
32 devices in a mesh: dp: 8 (over y, x, core), mp: 4 (over z).
Axes of the slice: x: 2, y: 2, z: 4, core: 2. Of those that a mesh axis runs over, the one named last changes fastest.
Arguments:
- states: bfloat16 [512, 64, 256], P('dp', 'mp'), may hold values from -6 to 6
- key_embed: bfloat16 [512, 128], P('dp'), may hold values from -6 to 6
- partner: int32 [512], replicated, may hold values from 0 to 511, as said below
- mix_numer: int32 [512], P('dp'), may hold values from 1 to 15
- lengths: int32 [512], replicated, may hold values from 8 to 64
- w_qkv: bfloat16 [3, 256, 256], P(None, None, 'mp'), may hold values from -0.375 to 0.375
- w_out: bfloat16 [256, 256], P('mp'), may hold values from -0.375 to 0.375
- w_up: bfloat16 [256, 1024], P(None, 'mp'), may hold values from -0.375 to 0.375
- w_down: bfloat16 [1024, 256], P('mp'), may hold values from -0.1875 to 0.1875
- w_proj: bfloat16 [256, 128], replicated, may hold values from -0.375 to 0.375
Outputs:
- session_loss: float32 [512], P('dp')
- grad_states: float32 [512, 64, 256], P('dp', 'mp')
Inputs may be any that keep to these rules, and one draw needn't show every extreme that they name: partner is a permutation of the 512 sessions; a session and its partner lie in different aligned blocks of 64 sessions, and at most 10 sessions of one block have their partners in one same other block.
All inputs are finite; a program needn't handle non-finite values.
Results may differ from a plain program's by a relative error of at most 0.0091.
Values may be sent and summed in bfloat16 or wider, within the bound.
A program may use at most 64 MiB of HBM per device.

v0:
```python
import jax
import jax.numpy as jnp
from jax import lax
from jax.sharding import PartitionSpec as P

HD = 64
SOFTMAX_TEMP = 0.1
LN_EPS = 1e-05
NORM_EPS = 1e-06
TOP_PRECISION = lax.Precision.HIGHEST


def swap_rows(buffer):
    return lax.all_to_all(buffer, "dp", split_axis=0, concat_axis=0, tiled=True)


def local(states, key_embed, partner, mix_numer, lengths, w_qkv, w_out, w_up, w_down, w_proj):
    sessions_dev, ev_part, width = states.shape
    n_data = lax.axis_size("dp")
    capacity = (sessions_dev + n_data - 2) // (n_data - 1)
    device_index = lax.axis_index("dp")
    model_index = lax.axis_index("mp")
    all_keys = lax.all_gather(key_embed, "dp", axis=0, tiled=True)
    session_count = partner.shape[0]
    local_ids = jnp.arange(sessions_dev, dtype=jnp.int32)
    own_ids = device_index * sessions_dev + local_ids
    own_partner = lax.dynamic_slice_in_dim(partner, device_index * sessions_dev, sessions_dev)
    mixup_weight = mix_numer.astype(jnp.float32) / 16.0
    source = own_partner // sessions_dev
    earlier = local_ids[None, :] < local_ids[:, None]
    in_slot = jnp.sum(((source[:, None] == source[None, :]) & earlier).astype(jnp.int32), axis=1)
    wanted = partner[None, :] == own_ids[:, None]
    seeker = jnp.sum(
        jnp.where(wanted, jnp.arange(session_count, dtype=jnp.int32)[None, :], 0), axis=1
    )
    target = seeker // sessions_dev
    seeker_rows = partner.reshape(n_data, sessions_dev)[target]
    out_slot = jnp.sum(
        (
            (seeker_rows // sessions_dev == device_index)
            & (local_ids[None, :] < (seeker % sessions_dev)[:, None])
        ).astype(jnp.int32),
        axis=1,
    )
    row_len = ev_part * width
    outgoing = (
        jnp.zeros((n_data, capacity, row_len), jnp.bfloat16)
        .at[target, out_slot]
        .set(states.reshape(sessions_dev, row_len))
    )
    incoming = swap_rows(outgoing)
    partner_states = incoming[source, in_slot].reshape(sessions_dev, ev_part, width)
    mix_rows = mixup_weight[:, None, None]
    mixed_part = (
        mix_rows * states.astype(jnp.float32)
        + (1.0 - mix_rows) * partner_states.astype(jnp.float32)
    ).astype(jnp.bfloat16)
    own_lengths = lax.dynamic_slice_in_dim(lengths, device_index * sessions_dev, sessions_dev)
    len_mix = jnp.maximum(own_lengths, lengths[own_partner])
    qkv_full, out_full, up_full, down_full = (w_qkv, w_out, w_up, w_down)
    mixed = lax.all_gather(mixed_part, "mp", axis=1, tiled=True)
    layer_sessions = mixed.shape[0]
    events = mixed.shape[1]
    rows = layer_sessions * events
    positions = jnp.arange(events, dtype=jnp.int32)
    token_mask = (positions[None, :] < len_mix[:, None]).astype(jnp.float32)
    pool_weights = token_mask / len_mix[:, None].astype(jnp.float32)
    inputs_f = mixed.astype(jnp.float32).reshape(rows, width)
    row_mean = jnp.mean(inputs_f, axis=1, keepdims=True)
    centered = inputs_f - row_mean
    inv_std = lax.rsqrt(jnp.mean(centered * centered, axis=1, keepdims=True) + LN_EPS)
    unit_rows = centered * inv_std
    normed = unit_rows.astype(jnp.bfloat16)
    projected = jnp.einsum(
        "rd,jdf->jrf", normed, qkv_full, preferred_element_type=jnp.float32
    ).astype(jnp.bfloat16)
    inner_part = qkv_full.shape[2]
    heads_part = inner_part // HD
    query_h = projected[0].reshape(layer_sessions, events, heads_part, HD)
    key_h = projected[1].reshape(layer_sessions, events, heads_part, HD)
    value_h = projected[2].reshape(layer_sessions, events, heads_part, HD)
    score_scale = HD ** (-0.5)
    scores = (
        jnp.einsum("sthc,srhc->shtr", query_h, key_h, preferred_element_type=jnp.float32)
        * score_scale
    )
    exp_scores = jnp.exp(scores) * token_mask[:, None, None, :]
    probs = exp_scores / jnp.sum(exp_scores, axis=3, keepdims=True)
    probs_b = probs.astype(jnp.bfloat16)
    context = (
        jnp.einsum("shtr,srhc->sthc", probs_b, value_h, preferred_element_type=jnp.float32)
        .astype(jnp.bfloat16)
        .reshape(rows, inner_part)
    )
    pre_act = jnp.dot(normed, up_full, preferred_element_type=jnp.float32)
    hidden = jax.nn.gelu(pre_act).astype(jnp.bfloat16)
    branch = jnp.dot(context, out_full, preferred_element_type=jnp.float32) + jnp.dot(
        hidden, down_full, preferred_element_type=jnp.float32
    )
    pooled_branch = jnp.einsum(
        "st,std->sd",
        pool_weights,
        branch.reshape(layer_sessions, events, width),
        precision=TOP_PRECISION,
    )
    pooled_input = jnp.einsum(
        "st,std->sd",
        pool_weights,
        inputs_f.reshape(layer_sessions, events, width),
        precision=TOP_PRECISION,
    )
    pooled = lax.psum(pooled_branch, "mp") + pooled_input
    proj_f = w_proj.astype(jnp.float32)
    embed = jnp.dot(pooled, proj_f, precision=TOP_PRECISION)
    inv_norm = lax.rsqrt(jnp.sum(embed * embed, axis=1, keepdims=True) + NORM_EPS)
    unit_query_rows = embed * inv_norm
    keys_f = all_keys.astype(jnp.float32)
    unit_key_rows = keys_f * lax.rsqrt(jnp.sum(keys_f * keys_f, axis=1, keepdims=True) + NORM_EPS)
    pair_logits = (
        jnp.einsum("an,qn->aq", unit_query_rows, unit_key_rows, precision=TOP_PRECISION)
        / SOFTMAX_TEMP
    )
    exp_logits = jnp.exp(pair_logits)
    sum_exp = jnp.sum(exp_logits, axis=1)
    own_logit = jnp.take_along_axis(pair_logits, own_ids[:, None], axis=1)[:, 0]
    partner_logit = jnp.take_along_axis(pair_logits, own_partner[:, None], axis=1)[:, 0]
    session_loss = (
        jnp.log(sum_exp) - mixup_weight * own_logit - (1.0 - mixup_weight) * partner_logit
    )
    normalized_exponent = exp_logits / sum_exp[:, None]
    unit_gradient = (
        jnp.dot(normalized_exponent, unit_key_rows, precision=TOP_PRECISION)
        - mixup_weight[:, None] * unit_key_rows[own_ids]
        - (1.0 - mixup_weight)[:, None] * unit_key_rows[own_partner]
    ) / SOFTMAX_TEMP
    grad_embed = (
        unit_gradient
        - unit_query_rows * jnp.sum(unit_query_rows * unit_gradient, axis=1, keepdims=True)
    ) * inv_norm
    grad_pooled = jnp.einsum("se,de->sd", grad_embed, proj_f, precision=TOP_PRECISION)
    grad_full = grad_pooled[:, None, :] * pool_weights[:, :, None]
    grad_b = grad_full.reshape(rows, width).astype(jnp.bfloat16)
    d_hidden = jnp.einsum("rd,fd->rf", grad_b, down_full, preferred_element_type=jnp.float32)
    d_pre = jax.vjp(jax.nn.gelu, pre_act)[1](d_hidden)[0].astype(jnp.bfloat16)
    d_context = (
        jnp.einsum("rd,fd->rf", grad_b, out_full, preferred_element_type=jnp.float32)
        .astype(jnp.bfloat16)
        .reshape(layer_sessions, events, heads_part, HD)
    )
    d_value = jnp.einsum(
        "shtr,sthc->srhc", probs_b, d_context, preferred_element_type=jnp.float32
    ).astype(jnp.bfloat16)
    d_prob = jnp.einsum("sthc,srhc->shtr", d_context, value_h, preferred_element_type=jnp.float32)
    d_score = (
        probs * (d_prob - jnp.sum(probs * d_prob, axis=3, keepdims=True)) * score_scale
    ).astype(jnp.bfloat16)
    d_query = jnp.einsum(
        "shtr,srhc->sthc", d_score, key_h, preferred_element_type=jnp.float32
    ).astype(jnp.bfloat16)
    d_key = jnp.einsum(
        "shtr,sthc->srhc", d_score, query_h, preferred_element_type=jnp.float32
    ).astype(jnp.bfloat16)
    d_proj = jnp.stack([d_query, d_key, d_value]).reshape(3, rows, inner_part)
    d_normed = jnp.einsum(
        "jrf,jdf->rd", d_proj, qkv_full, preferred_element_type=jnp.float32
    ) + jnp.einsum("rf,df->rd", d_pre, up_full, preferred_element_type=jnp.float32)
    d_normed = d_normed.reshape(layer_sessions, events, width)
    unit_all = unit_rows.reshape(layer_sessions, events, width)
    inv_all = inv_std.reshape(layer_sessions, events, 1)
    event_start = model_index * ev_part
    unit_part = lax.dynamic_slice_in_dim(unit_all, event_start, ev_part, 1)
    inv_part = lax.dynamic_slice_in_dim(inv_all, event_start, ev_part, 1)
    d_full = lax.psum(d_normed, "mp")
    d_local = lax.dynamic_slice_in_dim(d_full, event_start, ev_part, 1)
    center = jnp.mean(d_local, axis=2, keepdims=True)
    along = jnp.mean(d_local * unit_part, axis=2, keepdims=True)
    d_mixed = (
        lax.dynamic_slice_in_dim(grad_full, event_start, ev_part, 1)
        + (d_local - center - unit_part * along) * inv_part
    )
    d_mixed_rows = d_mixed.reshape(sessions_dev, row_len)
    back_rows = ((1.0 - mixup_weight)[:, None] * d_mixed_rows).astype(jnp.bfloat16)
    returning = (
        jnp.zeros((n_data, capacity, row_len), jnp.bfloat16).at[source, in_slot].set(back_rows)
    )
    arrived = swap_rows(returning)
    grad_states = mixup_weight[:, None] * d_mixed_rows + arrived[target, out_slot].astype(
        jnp.float32
    )
    return (session_loss, grad_states.reshape(sessions_dev, ev_part, width))


def solution(mesh):
    placed = (
        P("dp", "mp", None),
        P("dp", None),
        P(),
        P("dp"),
        P(),
        P(None, None, "mp"),
        P("mp", None),
        P(None, "mp"),
        P("mp", None),
        P(),
    )
    return jax.shard_map(
        local, mesh=mesh, in_specs=placed, out_specs=(P("dp"), P("dp", "mp", None)), check_vma=False
    )
```

profile of v0, /device:TPU:0, one launch (start us, length us, event | category | flops | bytes accessed | tf_op | source)
XLA Modules:
  0.0 415.0 jit_solution(1312834488764694528)
XLA Ops:
  12.3 9.7 %scatter_fusion = bf16[8,10,4096]{2,0,1:T(8,128)(2,1)S(1)} fusion(bf16[8,10,4096]{2,0,1:T(8,128)(2,1)S(1)} %broadcast.348.clone, s32[64]{0:T(128)S(1)} %get-tuple-element.15, bf16[64,4096]{1,0:T(8,128)(2,1)S(1)} %bitcast.216), kind=kCustom, calls=%fused_computation.8 | custom fusion | bytes 1573376 | tf_op jit(solution)/shard_map/scatter | solution.py:49
  23.4 5.2 %all-to-all-start = ((bf16[8,10,4096]{2,1,0:T(8,128)(2,1)}), bf16[8,10,4096]{2,1,0:T(8,128)(2,1)S(1)}, u32[]{:S(2)}, u32[]{:S(2)}) async-start(bf16[8,10,4096]{2,1,0:T(8,128)(2,1)} %copy.60), calls=%async_computation | async-start | bytes 2097152 | tf_op jit(solution)/shard_map/all_to_all | solution.py:14
  28.8 15.1 %all-to-all-done = bf16[8,10,4096]{2,1,0:T(8,128)(2,1)S(1)} async-done(((bf16[8,10,4096]{2,1,0:T(8,128)(2,1)}), bf16[8,10,4096]{2,1,0:T(8,128)(2,1)S(1)}, u32[]{:S(2)}, u32[]{:S(2)}) %all-to-all-start) | async-done | bytes 655392 | tf_op jit(solution)/shard_map/all_to_all | solution.py:14
  44.3 2.2 gather_fusion.2
  49.5 8.2 %all_gather.7 = bf16[512,128]{1,0:T(8,128)(2,1)S(1)} all-gather(bf16[64,128]{1,0:T(8,128)(2,1)S(1)} %copy-done.17), channel_id=1, replica_groups=mesh['dp'=8,'mp'=4] {'dp'}, dimensions={0}, use_global_device_ids=true | all-gather | bytes 147456 | tf_op jit(solution)/shard_map/all_gather | solution.py:23
  61.1 31.9 %all-gather.2.cloned.1.call-done = bf16[64,64,256]{2,1,0:T(8,128)(2,1)} async-done(((bf16[64,16,256]{2,1,0:T(8,128)(2,1)}), bf16[64,64,256]{2,1,0:T(8,128)(2,1)}) %all-gather.2.cloned.1.call-update) | async-done | bytes 2097168 | tf_op jit(solution)/shard_map/all_gather | solution.py:61
  93.0 2.4 convert_reduce_fusion
  95.4 3.1 broadcast_subtract_fusion
  98.6 2.5 fusion.10
  103.1 2.1 reshape.404
  105.1 2.1 reshape.403
  108.9 3.7 fusion.132
  112.6 5.0 %fusion.26 = (f32[64,64]{1,0:T(8,128)S(1)}, f32[64,64,64]{1,2,0:T(8,128)S(1)}) fusion(f32[64,64]{1,0:T(8,128)S(1)} %copy-done.15, bf16[64,64,64]{1,0,2:T(8,128)(2,1)S(1)} %copy-done.9, bf16[64,64,64]{1,0,2:T(8,128)(2,1)S(1)} %copy-done.7), kind=kOutput, calls=%fused_computation.48 | convolution fusion | flops 34336768 | bytes 2129920 | tf_op jit(solution)/shard_map/sthc,srhc->shtr/dot_general | solution.py:84
  122.7 1.9 convolution_add_fusion.1
  124.7 2.1 fusion.133
  129.2 31.5 %all-reduce.3.cloned.1.call-done = f32[64,256]{1,0:T(8,128)} async-done(((f32[64,256]{1,0:T(8,128)}), f32[64,256]{1,0:T(8,128)}) %all-reduce.3.cloned.1.call-update) | async-done | bytes 65552 | tf_op jit(solution)/shard_map/psum | solution.py:112
  167.9 2.8 reshape.407
  170.7 3.8 fusion.58
  174.5 3.4 fusion.45
  177.8 6.9 %fusion.49 = bf16[64,64,1,64]{1,3,0,2:T(8,128)(2,1)} fusion(f32[64,64,64]{1,2,0:T(8,128)} %fusion.58, bf16[64,64,64]{1,0,2:T(8,128)(2,1)} %reshape.404, f32[64,64,64]{1,2,0:T(8,128)} %copy-done.27, f32[64,64]{1,0:T(8,128)} %copy-done.29, f32[64,64]{1,0:T(8,128)} %fusion.80), kind=kOutput, calls=%fused_computation.64 | convolution fusion | flops 36704320 | bytes 3178496 | tf_op jit(solution)/shard_map/shtr,srhc->sthc/dot_general | solution.py:157
  184.7 7.8 %fusion.46 = bf16[64,64,1,64]{1,3,0,2:T(8,128)(2,1)} fusion(f32[64,64,64]{1,2,0:T(8,128)} %fusion.58, bf16[64,64,64]{1,0,2:T(8,128)(2,1)S(1)} %copy-done.8, f32[64,64,64]{1,2,0:T(8,128)} %copy-done.27, f32[64,64]{1,0:T(8,128)} %copy-done.29, f32[64,64]{1,0:T(8,128)} %fusion.80), kind=kOutput, calls=%fused_computation.63 | convolution fusion | flops 36704320 | bytes 3178496 | tf_op jit(solution)/shard_map/shtr,sthc->srhc/dot_general | solution.py:160
  192.5 1.9 copy.77
  196.1 1.9 copy.74
  203.1 4.1 convolution_bitcast_fusion
  207.3 7.0 %convolution_add_fusion = f32[4096,256]{1,0:T(8,128)} fusion(f32[4096,256]{1,0:T(8,128)} %convolution_bitcast_fusion, bf16[256,256]{1,0:T(8,128)(2,1)S(1)} %copy-done.11, f32[4096,256]{1,0:T(8,128)} %fusion.132, bf16[4096,256]{1,0:T(8,128)(2,1)S(1)} %fusion.8, bf16[256,256]{1,0:T(8,128)(2,1)S(1)} %copy-done), kind=kOutput, calls=%fused_computation.13 | convolution fusion | flops 1095761920 | bytes 14942208 | tf_op jit(solution)/shard_map/rf,df->rd/dot_general | solution.py:166
  214.4 154.6 %all-reduce.5.cloned.1.call-done = f32[64,64,256]{2,1,0:T(8,128)} async-done(((f32[64,64,256]{2,1,0:T(8,128)}), f32[64,64,256]{2,1,0:T(8,128)}) %all-reduce.5.cloned.1.call-update) | async-done | bytes 4194320 | tf_op jit(solution)/shard_map/psum | solution.py:173
  369.1 2.1 dynamic-slice_reduce_fusion
  371.2 2.0 multiply_add_fusion
  374.0 9.7 %scatter_fusion.1 = bf16[8,10,4096]{2,0,1:T(8,128)(2,1)S(1)} fusion(bf16[8,10,4096]{2,0,1:T(8,128)(2,1)S(1)} %broadcast.348, s32[64]{0:T(128)S(1)} %get-tuple-element.16, bf16[64,4096]{1,0:T(8,128)(2,1)S(1)} %multiply_convert_fusion.3), kind=kCustom, calls=%fused_computation.9 | custom fusion | bytes 1573376 | tf_op jit(solution)/shard_map/scatter | solution.py:184
  385.1 3.9 all-to-all-start.1
  391.4 13.0 %all-to-all-done.1 = bf16[8,10,4096]{2,1,0:T(8,128)(2,1)S(1)} async-done(((bf16[8,10,4096]{2,1,0:T(8,128)(2,1)}), bf16[8,10,4096]{2,1,0:T(8,128)(2,1)S(1)}, u32[]{:S(2)}, u32[]{:S(2)}) %all-to-all-start.1) | async-done | bytes 655392 | tf_op jit(solution)/shard_map/all_to_all | solution.py:14
  404.7 2.2 gather_fusion.5
  (143 shorter events, 44.6 us)
Async XLA Ops:
  7.2 114.1 %copy-start = (bf16[256,256]{1,0:T(8,128)(2,1)S(1)}, bf16[256,256]{1,0:T(8,128)(2,1)}, u32[]{:S(2)}) copy-start(bf16[256,256]{1,0:T(8,128)(2,1)} %param.20) | copy-start | bytes 393220
  22.0 6.8 %copy-start.25 = (s32[64]{0:T(128)S(1)}, s32[64]{0:T(128)}, u32[]{:S(2)}) copy-start(s32[64]{0:T(128)} %param.15) | copy-start | bytes 772
  23.4 20.6 %all-to-all-start = ((bf16[8,10,4096]{2,1,0:T(8,128)(2,1)}), bf16[8,10,4096]{2,1,0:T(8,128)(2,1)S(1)}, u32[]{:S(2)}, u32[]{:S(2)}) async-start(bf16[8,10,4096]{2,1,0:T(8,128)(2,1)} %copy.60), calls=%async_computation | async-start | bytes 2097152 | tf_op jit(solution)/shard_map/all_to_all | solution.py:14
  28.6 64.4 %all-gather.2.cloned.1.call-start = ((), (), s32[]{:S(2)}) async-start(), calls=%async_computation.2 | async-start | bytes 2621440 | tf_op jit(solution)/shard_map/all_gather | solution.py:61
  28.8 17.9 %copy-start.21 = (f32[64]{0:T(128)}, f32[64]{0:T(128)S(1)}, u32[]{:S(2)}) copy-start(f32[64]{0:T(128)S(1)} %get-tuple-element.21) | copy-start | bytes 772
  28.8 17.9 %copy-start.23 = (f32[64]{0:T(128)}, f32[64]{0:T(128)S(1)}, u32[]{:S(2)}) copy-start(f32[64]{0:T(128)S(1)} %get-tuple-element.20) | copy-start | bytes 772
  44.3 2.4 copy-start.6
  46.5 3.0 copy-start.17
  47.8 112.9 %all-reduce.3.cloned.1.call-start = ((), (), s32[]{:S(2)}) async-start(), calls=%async_computation.3 | async-start | bytes 131072 | tf_op jit(solution)/shard_map/psum | solution.py:112
  93.0 2.4 copy-start.2
  98.6 2.5 copy-start.14
  108.8 3.8 copy-start.7
  108.8 3.8 copy-start.9
  108.8 3.8 copy-start.15
  119.0 1.5 copy-start.12
  120.5 2.2 copy-start.4
  124.7 3.0 copy-start.3
  127.4 33.3 %copy-start.10 = (bf16[256,128]{1,0:T(8,128)(2,1)S(1)}, bf16[256,128]{1,0:T(8,128)(2,1)}, u32[]{:S(2)}) copy-start(bf16[256,128]{1,0:T(8,128)(2,1)} %param.21) | copy-start | bytes 196612
  127.4 241.6 %all-reduce.5.cloned.1.call-start = ((), (), s32[]{:S(2)}) async-start(), calls=%async_computation.4 | async-start | bytes 8388608 | tf_op jit(solution)/shard_map/psum | solution.py:173
  160.7 5.6 %copy-start.13 = (bf16[64,256]{1,0:T(8,128)(2,1)S(1)}, bf16[64,256]{1,0:T(8,128)(2,1)}, u32[]{:S(2)}) copy-start(bf16[64,256]{1,0:T(8,128)(2,1)} %param.18) | copy-start | bytes 98308
  170.7 3.8 copy-start.5
  170.7 3.8 copy-start.16
  170.7 3.8 copy-start.28
  170.7 3.8 copy-start.30
  177.8 6.9 %copy-start.8 = (bf16[64,64,64]{1,0,2:T(8,128)(2,1)S(1)}, bf16[64,64,64]{1,0,2:T(8,128)(2,1)}, u32[]{:S(2)}) copy-start(bf16[64,64,64]{1,0,2:T(8,128)(2,1)} %reshape.403) | copy-start | bytes 1572868
  203.1 4.1 copy-start.11
  371.2 2.6 copy-start.22
  383.7 5.4 %copy-start.20 = (s32[64,1,1]{0,2,1:T(1,128)S(1)}, s32[64,1,1]{0,2,1:T(1,128)}, u32[]{:S(2)}) copy-start(s32[64,1,1]{0,2,1:T(1,128)} %get-tuple-element.5) | copy-start | bytes 772
  383.7 7.2 %copy-start.19 = (f32[64]{0:T(128)S(1)}, f32[64]{0:T(128)}, u32[]{:S(2)}) copy-start(f32[64]{0:T(128)} %copy-done.18) | copy-start | bytes 772
  383.7 7.2 %copy-start.26 = (s32[64]{0:T(128)S(1)}, s32[64]{0:T(128)}, u32[]{:S(2)}) copy-start(s32[64]{0:T(128)} %param.15) | copy-start | bytes 772
  385.1 19.3 %all-to-all-start.1 = ((bf16[8,10,4096]{2,1,0:T(8,128)(2,1)}), bf16[8,10,4096]{2,1,0:T(8,128)(2,1)S(1)}, u32[]{:S(2)}, u32[]{:S(2)}) async-start(bf16[8,10,4096]{2,1,0:T(8,128)(2,1)} %copy.78), calls=%async_computation.1 | async-start | bytes 2097152 | tf_op jit(solution)/shard_map/all_to_all | solution.py:14
  404.7 2.4 copy-start.24
  (4 other events, 5.3 us)
Sparse Core Ops, SparseCore 0:
  47.9 45.0 all-gather.1
  127.6 33.0 all-reduce.2
  214.4 154.6 all-reduce.4
where the time goes:
time: 422 us; the launch traced here: 415 us
  waiting for transfers between devices  246 us (58%)
  local copies, waits for them, and re-layouts  60.4 us (14%)
  matrix products  55.9 us (13%)
  other arithmetic  20.1 us (5%)
  between operations  14.7 us (3%)
  starting transfers between devices  9.43 us (2%)
  blocking collectives  8.24 us (2%)
    psum x1, waiting for transfers between devices, local(): d_full = lax.psum(d_normed, 'mp')  155 us
    all_gather x1, waiting for transfers between devices, local(): mixed = lax.all_gather(mixed_part, 'mp', axis=1, tiled=True)  31.9 us
    psum x1, waiting for transfers between devices, local(): pooled = lax.psum(pooled_branch, 'mp') + pooled_input  31.5 us
    all_to_all x2, waiting for transfers between devices, swap_rows(): return lax.all_to_all(buffer, 'dp', split_axis=0, concat_axis=0, tiled=True)  28.1 us
    scatter x2, local copies, waits for them, and re-layouts, local(): outgoing = jnp.zeros((n_data, capacity, row_len), jnp.bfloat16).at[target...  11.1 us
    scatter x2, local copies, waits for them, and re-layouts, local(): jnp.zeros((n_data, capacity, row_len), jnp.bfloat16).at[source, in_slot]  11.1 us
    all_to_all x2, starting transfers between devices, swap_rows(): return lax.all_to_all(buffer, 'dp', split_axis=0, concat_axis=0, tiled=True)  9.13 us
    another operation x6, local copies, waits for them, and re-layouts  8.6 us
  transfers between devices with their start and end apart: 5, of which 5 were waited for; matrix products, arithmetic and copies ran while one was open for 2% of the time, Pallas kernels for 0%

commit v1 on v0

--- a/solution.py
+++ b/solution.py
@@ -2,6 +2,7 @@
 import jax.numpy as jnp
 from jax import lax
 from jax.sharding import PartitionSpec as P
+from jax.lax import all_gather
 
 HD = 64
 SOFTMAX_TEMP = 0.1
@@ -109,7 +110,7 @@
         inputs_f.reshape(layer_sessions, events, width),
         precision=TOP_PRECISION,
     )
-    pooled = lax.psum(pooled_branch, "mp") + pooled_input
+    pooled = jnp.sum(all_gather(pooled_branch, "mp"), 0) + pooled_input
     proj_f = w_proj.astype(jnp.float32)
     embed = jnp.dot(pooled, proj_f, precision=TOP_PRECISION)
     inv_norm = lax.rsqrt(jnp.sum(embed * embed, axis=1, keepdims=True) + NORM_EPS)

time: 422 us -> 402 us (0.953)
  waiting for transfers between devices: 246 us -> 214 us
  blocking collectives: 8.24 us -> 23.2 us
    psum x1 -> x0, waiting for transfers between devices: 31.5 us -> none  [local(): pooled = lax.psum(pooled_branch, 'mp') + pooled_input]
    all_gather x0 -> x1, blocking collectives: none -> 14.9 us  [local(): pooled = jnp.sum(all_gather(pooled_branch, 'mp'), 0) + pooled_input]
  transfers between devices with their start and end apart: 5 -> 4, of which waited for: 5 -> 4; matrix products, arithmetic and copies ran while one was open for 2% -> 2% of each run, Pallas kernels for 0% -> 0%
where the time goes in v1:
time: 402 us; the launch traced here: 395 us
  waiting for transfers between devices  214 us (53%)
  local copies, waits for them, and re-layouts  59.9 us (15%)
  matrix products  53.3 us (13%)
  blocking collectives  23.2 us (6%)
  other arithmetic  21 us (5%)
  between operations  15.1 us (4%)
  starting transfers between devices  9.21 us (2%)
    psum x1, waiting for transfers between devices, local(): d_full = lax.psum(d_normed, 'mp')  154 us
    all_gather x1, waiting for transfers between devices, local(): mixed = lax.all_gather(mixed_part, 'mp', axis=1, tiled=True)  31.9 us
    all_to_all x2, waiting for transfers between devices, swap_rows(): return lax.all_to_all(buffer, 'dp', split_axis=0, concat_axis=0, tiled=True)  28.1 us
    all_gather x1, blocking collectives, local(): pooled = jnp.sum(all_gather(pooled_branch, 'mp'), 0) + pooled_input  14.9 us
    scatter x2, local copies, waits for them, and re-layouts, local(): outgoing = jnp.zeros((n_data, capacity, row_len), jnp.bfloat16).at[target...  11.1 us
    scatter x2, local copies, waits for them, and re-layouts, local(): jnp.zeros((n_data, capacity, row_len), jnp.bfloat16).at[source, in_slot]  11.1 us
    all_to_all x2, starting transfers between devices, swap_rows(): return lax.all_to_all(buffer, 'dp', split_axis=0, concat_axis=0, tiled=True)  9.13 us
    another operation x6, local copies, waits for them, and re-layouts  8.59 us
  transfers between devices with their start and end apart: 4, of which 4 were waited for; matrix products, arithmetic and copies ran while one was open for 2% of the time, Pallas kernels for 0%

profile of v1, /device:TPU:0, one launch (start us, length us, event | category | flops | bytes accessed | tf_op | source)
XLA Modules:
  0.0 395.5 jit_solution(7527070246258354773)
XLA Ops:
  12.3 9.7 %scatter_fusion = bf16[8,10,4096]{2,0,1:T(8,128)(2,1)S(1)} fusion(bf16[8,10,4096]{2,0,1:T(8,128)(2,1)S(1)} %broadcast.348.clone, s32[64]{0:T(128)S(1)} %get-tuple-element.15, bf16[64,4096]{1,0:T(8,128)(2,1)S(1)} %bitcast.217), kind=kCustom, calls=%fused_computation.8 | custom fusion | bytes 1573376 | tf_op jit(solution)/shard_map/scatter | solution.py:50
  23.4 5.2 %all-to-all-start = ((bf16[8,10,4096]{2,1,0:T(8,128)(2,1)}), bf16[8,10,4096]{2,1,0:T(8,128)(2,1)S(1)}, u32[]{:S(2)}, u32[]{:S(2)}) async-start(bf16[8,10,4096]{2,1,0:T(8,128)(2,1)} %copy.60), calls=%async_computation | async-start | bytes 2097152 | tf_op jit(solution)/shard_map/all_to_all | solution.py:15
  28.8 15.1 %all-to-all-done = bf16[8,10,4096]{2,1,0:T(8,128)(2,1)S(1)} async-done(((bf16[8,10,4096]{2,1,0:T(8,128)(2,1)}), bf16[8,10,4096]{2,1,0:T(8,128)(2,1)S(1)}, u32[]{:S(2)}, u32[]{:S(2)}) %all-to-all-start) | async-done | bytes 655392 | tf_op jit(solution)/shard_map/all_to_all | solution.py:15
  44.3 2.2 gather_fusion.2
  49.5 8.2 %all_gather.15 = bf16[512,128]{1,0:T(8,128)(2,1)S(1)} all-gather(bf16[64,128]{1,0:T(8,128)(2,1)S(1)} %copy-done.22), channel_id=1, replica_groups=mesh['dp'=8,'mp'=4] {'dp'}, dimensions={0}, use_global_device_ids=true | all-gather | bytes 147456 | tf_op jit(solution)/shard_map/all_gather | solution.py:24
  61.1 31.9 %all-gather.3.cloned.1.call-done = bf16[64,64,256]{2,1,0:T(8,128)(2,1)} async-done(((bf16[64,16,256]{2,1,0:T(8,128)(2,1)}), bf16[64,64,256]{2,1,0:T(8,128)(2,1)}) %all-gather.3.cloned.1.call-update) | async-done | bytes 2097168 | tf_op jit(solution)/shard_map/all_gather | solution.py:62
  93.0 2.4 convert_reduce_fusion
  95.4 3.1 broadcast_subtract_fusion
  98.6 2.5 fusion.10
  103.1 2.1 reshape.404
  105.2 2.2 reshape.403
  108.9 3.7 fusion.132
  112.6 5.0 %fusion.26 = (f32[64,64]{1,0:T(8,128)S(1)}, f32[64,64,64]{1,2,0:T(8,128)S(1)}) fusion(f32[64,64]{1,0:T(8,128)S(1)} %copy-done.20, bf16[64,64,64]{1,0,2:T(8,128)(2,1)S(1)} %copy-done.9, bf16[64,64,64]{1,0,2:T(8,128)(2,1)S(1)} %copy-done.7), kind=kOutput, calls=%fused_computation.48 | convolution fusion | flops 34336768 | bytes 2129920 | tf_op jit(solution)/shard_map/sthc,srhc->shtr/dot_general | solution.py:85
  122.7 1.9 convolution_add_fusion.1
  124.7 2.1 fusion.133
  126.8 14.9 %all-gather = f32[256,256]{1,0:T(8,128)} all-gather(f32[64,256]{1,0:T(8,128)S(1)} %bitcast.222), channel_id=2, replica_groups=mesh['dp'=8,'mp'=4] {'mp'}, dimensions={0}, use_global_device_ids=true | all-gather | bytes 327680 | tf_op jit(solution)/shard_map/all_gather | solution.py:113
  149.0 2.7 reshape.407
  151.7 3.8 fusion.58
  155.5 3.4 fusion.45
  158.9 6.9 %fusion.49 = bf16[64,64,1,64]{1,3,0,2:T(8,128)(2,1)} fusion(f32[64,64,64]{1,2,0:T(8,128)} %fusion.58, bf16[64,64,64]{1,0,2:T(8,128)(2,1)} %reshape.404, f32[64,64,64]{1,2,0:T(8,128)} %copy-done.32, f32[64,64]{1,0:T(8,128)} %copy-done.34, f32[64,64]{1,0:T(8,128)} %fusion.80), kind=kOutput, calls=%fused_computation.64 | convolution fusion | flops 36704320 | bytes 3178496 | tf_op jit(solution)/shard_map/shtr,srhc->sthc/dot_general | solution.py:158
  165.8 7.7 %fusion.46 = bf16[64,64,1,64]{1,3,0,2:T(8,128)(2,1)} fusion(f32[64,64,64]{1,2,0:T(8,128)} %fusion.58, bf16[64,64,64]{1,0,2:T(8,128)(2,1)S(1)} %copy-done.8, f32[64,64,64]{1,2,0:T(8,128)} %copy-done.32, f32[64,64]{1,0:T(8,128)} %copy-done.34, f32[64,64]{1,0:T(8,128)} %fusion.80), kind=kOutput, calls=%fused_computation.63 | convolution fusion | flops 36704320 | bytes 3178496 | tf_op jit(solution)/shard_map/shtr,sthc->srhc/dot_general | solution.py:161
  173.5 1.9 copy.77
  177.0 1.9 copy.74
  184.1 4.2 %convolution_bitcast_fusion = f32[4096,256]{1,0:T(8,128)} fusion(bf16[3,256,64]{1,2,0:T(8,128)(2,1)} %param.17, bf16[1,4096,64]{1,2,0:T(8,128)(2,1)} %stack.14, bf16[1,4096,64]{1,2,0:T(8,128)(2,1)} %stack.13, bf16[1,4096,64]{1,2,0:T(8,128)(2,1)} %stack.12), kind=kOutput, calls=%fused_computation.14 | convolution fusion | flops 404226048 | bytes 5865472 | tf_op jit(solution)/shard_map/jrf,jdf->rd/dot_general | solution.py:165
  188.2 7.0 %convolution_add_fusion = f32[4096,256]{1,0:T(8,128)} fusion(f32[4096,256]{1,0:T(8,128)} %convolution_bitcast_fusion, bf16[256,256]{1,0:T(8,128)(2,1)S(1)} %copy-done.13, f32[4096,256]{1,0:T(8,128)} %fusion.132, bf16[4096,256]{1,0:T(8,128)(2,1)S(1)} %fusion.8, bf16[256,256]{1,0:T(8,128)(2,1)S(1)} %copy-done), kind=kOutput, calls=%fused_computation.13 | convolution fusion | flops 1095761920 | bytes 14942208 | tf_op jit(solution)/shard_map/rf,df->rd/dot_general | solution.py:167
  195.4 153.8 %all-reduce.2.cloned.1.call-done = f32[64,64,256]{2,1,0:T(8,128)} async-done(((f32[64,64,256]{2,1,0:T(8,128)}), f32[64,64,256]{2,1,0:T(8,128)}) %all-reduce.2.cloned.1.call-update) | async-done | bytes 4194320 | tf_op jit(solution)/shard_map/psum | solution.py:174
  349.2 2.1 dynamic-slice_reduce_fusion
  351.3 2.0 multiply_add_fusion
  354.1 9.7 %scatter_fusion.1 = bf16[8,10,4096]{2,0,1:T(8,128)(2,1)S(1)} fusion(bf16[8,10,4096]{2,0,1:T(8,128)(2,1)S(1)} %broadcast.348, s32[64]{0:T(128)S(1)} %get-tuple-element.16, bf16[64,4096]{1,0:T(8,128)(2,1)S(1)} %multiply_convert_fusion.3), kind=kCustom, calls=%fused_computation.9 | custom fusion | bytes 1573376 | tf_op jit(solution)/shard_map/scatter | solution.py:185
  365.2 3.9 all-to-all-start.1
  371.5 13.0 %all-to-all-done.1 = bf16[8,10,4096]{2,1,0:T(8,128)(2,1)S(1)} async-done(((bf16[8,10,4096]{2,1,0:T(8,128)(2,1)}), bf16[8,10,4096]{2,1,0:T(8,128)(2,1)S(1)}, u32[]{:S(2)}, u32[]{:S(2)}) %all-to-all-start.1) | async-done | bytes 655392 | tf_op jit(solution)/shard_map/all_to_all | solution.py:15
  384.9 2.2 gather_fusion.5
  (152 shorter events, 42.1 us)
Async XLA Ops:
  7.2 114.2 %copy-start = (bf16[256,256]{1,0:T(8,128)(2,1)S(1)}, bf16[256,256]{1,0:T(8,128)(2,1)}, u32[]{:S(2)}) copy-start(bf16[256,256]{1,0:T(8,128)(2,1)} %param.20) | copy-start | bytes 393220
  22.0 6.8 %copy-start.30 = (s32[64]{0:T(128)S(1)}, s32[64]{0:T(128)}, u32[]{:S(2)}) copy-start(s32[64]{0:T(128)} %param.15) | copy-start | bytes 772
  23.4 20.6 %all-to-all-start = ((bf16[8,10,4096]{2,1,0:T(8,128)(2,1)}), bf16[8,10,4096]{2,1,0:T(8,128)(2,1)S(1)}, u32[]{:S(2)}, u32[]{:S(2)}) async-start(bf16[8,10,4096]{2,1,0:T(8,128)(2,1)} %copy.60), calls=%async_computation | async-start | bytes 2097152 | tf_op jit(solution)/shard_map/all_to_all | solution.py:15
  28.6 64.4 %all-gather.3.cloned.1.call-start = ((), (), s32[]{:S(2)}) async-start(), calls=%async_computation.2 | async-start | bytes 2621440 | tf_op jit(solution)/shard_map/all_gather | solution.py:62
  28.8 17.9 %copy-start.26 = (f32[64]{0:T(128)}, f32[64]{0:T(128)S(1)}, u32[]{:S(2)}) copy-start(f32[64]{0:T(128)S(1)} %get-tuple-element.21) | copy-start | bytes 772
  28.8 17.9 %copy-start.28 = (f32[64]{0:T(128)}, f32[64]{0:T(128)S(1)}, u32[]{:S(2)}) copy-start(f32[64]{0:T(128)S(1)} %get-tuple-element.20) | copy-start | bytes 772
  44.3 2.4 copy-start.6
  46.5 3.0 copy-start.22
  47.8 301.4 %all-reduce.2.cloned.1.call-start = ((), (), s32[]{:S(2)}) async-start(), calls=%async_computation.3 | async-start | bytes 8388608 | tf_op jit(solution)/shard_map/psum | solution.py:174
  93.0 2.4 copy-start.2
  98.6 2.5 copy-start.16
  108.8 3.8 copy-start.7
  108.8 3.8 copy-start.9
  108.9 3.8 copy-start.20
  120.6 2.2 copy-start.4
  124.7 18.7 %copy-start.3 = (bf16[64,64,256]{2,1,0:T(8,128)(2,1)S(1)}, bf16[64,64,256]{2,1,0:T(8,128)(2,1)}, u32[]{:S(2)}) copy-start(bf16[64,64,256]{2,1,0:T(8,128)(2,1)} %all-gather.3.cloned.1.call-done) | copy-start | bytes 6291460
  126.8 17.5 %copy-start.10 = (bf16[256,128]{1,0:T(8,128)(2,1)S(1)}, bf16[256,128]{1,0:T(8,128)(2,1)}, u32[]{:S(2)}) copy-start(bf16[256,128]{1,0:T(8,128)(2,1)} %param.21) | copy-start | bytes 196612
  143.3 3.0 copy-start.11
  143.4 3.3 copy-start.17
  144.3 3.1 copy-start.15
  151.7 3.8 copy-start.5
  151.7 3.8 copy-start.21
  151.7 3.8 copy-start.33
  151.7 3.8 copy-start.35
  158.9 6.9 %copy-start.8 = (bf16[64,64,64]{1,0,2:T(8,128)(2,1)S(1)}, bf16[64,64,64]{1,0,2:T(8,128)(2,1)}, u32[]{:S(2)}) copy-start(bf16[64,64,64]{1,0,2:T(8,128)(2,1)} %reshape.403) | copy-start | bytes 1572868
  184.1 4.2 %copy-start.13 = (bf16[256,256]{1,0:T(8,128)(2,1)S(1)}, bf16[256,256]{1,0:T(8,128)(2,1)}, u32[]{:S(2)}) copy-start(bf16[256,256]{1,0:T(8,128)(2,1)} %param.19) | copy-start | bytes 393220
  351.3 2.6 copy-start.27
  363.8 5.4 %copy-start.25 = (s32[64,1,1]{0,2,1:T(1,128)S(1)}, s32[64,1,1]{0,2,1:T(1,128)}, u32[]{:S(2)}) copy-start(s32[64,1,1]{0,2,1:T(1,128)} %get-tuple-element.5) | copy-start | bytes 772
  363.8 7.2 %copy-start.24 = (f32[64]{0:T(128)S(1)}, f32[64]{0:T(128)}, u32[]{:S(2)}) copy-start(f32[64]{0:T(128)} %copy-done.23) | copy-start | bytes 772
  363.8 7.2 %copy-start.31 = (s32[64]{0:T(128)S(1)}, s32[64]{0:T(128)}, u32[]{:S(2)}) copy-start(s32[64]{0:T(128)} %param.15) | copy-start | bytes 772
  365.2 19.3 %all-to-all-start.1 = ((bf16[8,10,4096]{2,1,0:T(8,128)(2,1)}), bf16[8,10,4096]{2,1,0:T(8,128)(2,1)S(1)}, u32[]{:S(2)}, u32[]{:S(2)}) async-start(bf16[8,10,4096]{2,1,0:T(8,128)(2,1)} %copy.78), calls=%async_computation.1 | async-start | bytes 2097152 | tf_op jit(solution)/shard_map/all_to_all | solution.py:15
  384.9 2.4 copy-start.29
  (8 other events, 11.5 us)
Sparse Core Ops, SparseCore 0:
  47.9 45.0 all-gather.2
  195.4 153.8 all-reduce.1
